TPU v7x, 32 devices: a whole 2x2x4 slice. The times are simulated.
32 devices in a mesh: row: 8 (over y, x, core), col: 4 (over z).
Axes of the slice: x: 2, y: 2, z: 4, core: 2. Of those that a mesh axis runs over, the one named last changes fastest.
Arguments:
- contact_map: bfloat16 [512, 512, 128], P('row', 'col'), may hold values from -6 to 6
- conv_weight: bfloat16 [2, 3, 3, 3, 128, 128], replicated, may hold values from -0.1875 to 0.1875
- conv_bias: float32 [2, 3, 128], replicated, may hold values from -0.5 to 0.5
Outputs:
- trunk_out: bfloat16 [512, 512, 128], P('row', 'col')
All inputs are finite; a program needn't handle non-finite values.
Results may differ from a plain program's by a relative error of at most 0.0085.
Values may be sent and summed in bfloat16 or wider, within the bound.
A program may use at most 128 MiB of HBM per device.

v0:
```python
import jax
import jax.numpy as jnp
from jax import lax
from jax.sharding import PartitionSpec as P


def with_halo(array, sides, width):
    for axis, dim in sides:
        devices, length = (lax.axis_size(axis), array.shape[dim])
        up = [(i, (i + 1) % devices) for i in range(devices - 1)]
        down = [(j, i) for i, j in up]
        last = lax.slice_in_dim(array, length - width, length, axis=dim)
        initial = lax.slice_in_dim(array, 0, width, axis=dim)
        before = lax.ppermute(last, axis, up)
        after = lax.ppermute(initial, axis, down)
        array = jnp.concatenate([before, array, after], axis=dim)
    return array


def convolve(padded, kernel, rows, cols, dilation):
    total = jnp.zeros((rows, cols, kernel.shape[3]), jnp.float32)
    for tap_row in range(3):
        for tap_col in range(3):
            piece = padded[
                tap_row * dilation : tap_row * dilation + rows,
                tap_col * dilation : tap_col * dilation + cols,
            ]
            total = total + jnp.dot(
                piece, kernel[tap_row, tap_col], preferred_element_type=jnp.float32
            )
    return total


def average(current, flipped):
    return ((current.astype(jnp.float32) + flipped.astype(jnp.float32)) * 0.5).astype(jnp.bfloat16)


def strip_pad(hidden, dilation):
    widened = jnp.pad(hidden, ((0, 0), (dilation, dilation), (0, 0)))
    return with_halo(widened, ((("row", "col"), 0),), dilation)


def run_block(current, flipped, conv_weight, conv_bias, block, padder):
    rows, cols = (current.shape[0], current.shape[1])
    mirrored = average(current, flipped)
    hidden = mirrored
    result = mirrored
    for layer, dilation in enumerate((1, 2, 4)):
        padded = padder(hidden, dilation)
        total = (
            convolve(padded, conv_weight[block, layer], rows, cols, dilation)
            + conv_bias[block, layer]
        )
        if layer < 2:
            hidden = jax.nn.relu(total).astype(jnp.bfloat16)
        else:
            result = (mirrored.astype(jnp.float32) + total).astype(jnp.bfloat16)
    return result


def per_device(contact_map, conv_weight, conv_bias):
    blocks = conv_weight.shape[0]
    current = lax.all_to_all(contact_map, "col", split_axis=0, concat_axis=1, tiled=True)
    for block in range(blocks):
        columns = lax.all_to_all(current, ("row", "col"), split_axis=1, concat_axis=0, tiled=True)
        flipped = jnp.transpose(columns, (1, 0, 2))
        current = run_block(current, flipped, conv_weight, conv_bias, block, strip_pad)
    return lax.all_to_all(current, "col", split_axis=1, concat_axis=0, tiled=True)


def solution(mesh):
    in_specs = (P("row", "col", None), P(), P())
    out_specs = P("row", "col", None)
    return jax.shard_map(
        per_device, mesh=mesh, in_specs=in_specs, out_specs=out_specs, check_vma=False
    )
```

profile of v0, /device:TPU:0, one launch (start us, length us, event | category | flops | bytes accessed | tf_op | source)
XLA Modules:
  0.0 503.3 jit_solution(15225654004325715221)
XLA Ops:
  0.0 54.5 %all_to_all.54 = bf16[64,128,128]{2,1,0:T(8,128)(2,1)S(1)} all-to-all(bf16[64,128,128]{2,1,0:T(8,128)(2,1)} %param.3), channel_id=1, replica_groups=mesh['row'=8,'col'=4] {'col'}, dimensions={0} | all-to-all | bytes 4194304 | tf_op jit(solution)/shard_map/all_to_all | solution.py:63
  54.7 2.7 copy.9
  57.3 4.0 all-to-all-start.1
  64.2 44.6 %all-to-all-done.1 = bf16[16,512,128]{2,0,1:T(8,128)(2,1)} async-done(((bf16[16,512,128]{2,0,1:T(8,128)(2,1)}), bf16[16,512,128]{2,0,1:T(8,128)(2,1)}, u32[]{:S(2)}, u32[]{:S(2)}) %all-to-all-start.1) | async-done | bytes 2097184 | tf_op jit(solution)/shard_map/all_to_all | solution.py:65
  119.2 2.7 fusion.128
  121.9 6.2 %collective-permute-start = (bf16[1,514,128]{2,1,0:T(8,128)(2,1)S(1)}, bf16[1,514,128]{2,1,0:T(8,128)(2,1)S(1)}, u32[]{:S(2)}, u32[]{:S(2)}) collective-permute-start(bf16[1,514,128]{2,1,0:T(8,128)(2,1)S(1)} %get-tuple-element.7), channel_id=1, source_target_pairs={{0,1},{1,2},{2,3},{3,4},{4,5},{5,6},{6,7},{7,8},{8,9},{9,10},{10,1... | collective-permute-start | bytes 394760 | tf_op jit(solution)/shard_map/ppermute | solution.py:14
  131.3 2.7 fusion.68
  134.0 2.7 fusion.74
  139.3 2.7 fusion.104
  142.1 11.9 %maximum_convert_fusion.3 = bf16[16,512,128]{2,1,0:T(8,128)(2,1)S(1)} fusion(f32[16,512,128]{2,1,0:T(8,128)} %fusion.65, f32[16,512,128]{2,1,0:T(8,128)} %fusion.68, f32[16,512,128]{2,1,0:T(8,128)} %fusion.128, f32[16,512,128]{2,1,0:T(8,128)} %fusion.145, f32[16,512,128]{2,1,0:T(8,128)} %fusion.130, f32[16,512,128]{2,1,0:T(8,128)} %fusion.104, ...), kind=kOutput, calls=%fused_computation.11 | convolution fusion | flops 284164096 | bytes 37947904 | tf_op jit(solution)/shard_map/dot_general | solution.py:28
  160.4 3.9 collective-permute-start.2
  165.8 2.7 fusion.124
  168.5 10.3 %collective-permute-done.3 = bf16[2,516,128]{2,1,0:T(8,128)(2,1)S(1)} collective-permute-done((bf16[2,516,128]{2,1,0:T(8,128)(2,1)S(1)}, bf16[2,516,128]{2,1,0:T(8,128)(2,1)S(1)}, u32[]{:S(2)}, u32[]{:S(2)}) %collective-permute-start.3) | collective-permute-done | bytes 264224 | tf_op jit(solution)/shard_map/ppermute | solution.py:15
  181.4 2.7 fusion.20
  184.2 2.7 fusion.26
  186.8 2.7 fusion.23
  189.5 2.7 fusion.98
  192.2 11.9 %maximum_convert_fusion.2 = bf16[16,512,128]{2,1,0:T(8,128)(2,1)S(1)} fusion(f32[16,512,128]{2,1,0:T(8,128)} %fusion.17, f32[16,512,128]{2,1,0:T(8,128)} %fusion.20, f32[16,512,128]{2,1,0:T(8,128)} %fusion.124, f32[16,512,128]{2,1,0:T(8,128)} %fusion.144, f32[16,512,128]{2,1,0:T(8,128)} %fusion.126, f32[16,512,128]{2,1,0:T(8,128)} %fusion.98, ...), kind=kOutput, calls=%fused_computation.10 | convolution fusion | flops 284164096 | bytes 38081024 | tf_op jit(solution)/shard_map/dot_general | solution.py:28
  208.4 2.7 fusion.120
  211.6 4.8 collective-permute-start.4
  223.1 2.7 fusion.44
  227.4 2.7 fusion.50
  232.7 2.7 fusion.94
  235.4 11.8 %add_convert_fusion.1 = bf16[16,512,128]{2,1,0:T(8,128)(2,1)S(1)} fusion(f32[16,512,128]{2,1,0:T(8,128)} %fusion.41, f32[16,512,128]{2,1,0:T(8,128)} %fusion.44, f32[16,512,128]{2,1,0:T(8,128)} %fusion.120, f32[16,512,128]{2,1,0:T(8,128)} %fusion.143, f32[16,512,128]{2,1,0:T(8,128)} %fusion.122, f32[16,512,128]{2,1,0:T(8,128)} %fusion.94, ...), kind=kOutput, calls=%fused_computation.9 | convolution fusion | flops 285212672 | bytes 40444416 | tf_op jit(solution)/shard_map/dot_general | solution.py:28
  248.6 59.4 %all_to_all.55 = bf16[16,512,128]{2,0,1:T(8,128)(2,1)S(1)} all-to-all(bf16[16,512,128]{2,0,1:T(8,128)(2,1)S(1)} %copy.11), channel_id=1, replica_groups=mesh['row'=8,'col'=4] {'row','col'}, dimensions={1} | all-to-all | bytes 4194304 | tf_op jit(solution)/shard_map/all_to_all | solution.py:65
  315.7 2.7 fusion.116
  319.0 6.0 %collective-permute-start.6 = (bf16[1,514,128]{2,1,0:T(8,128)(2,1)S(1)}, bf16[1,514,128]{2,1,0:T(8,128)(2,1)S(1)}, u32[]{:S(2)}, u32[]{:S(2)}) collective-permute-start(bf16[1,514,128]{2,1,0:T(8,128)(2,1)S(1)} %get-tuple-element.5), channel_id=1, source_target_pairs={{0,1},{1,2},{2,3},{3,4},{4,5},{5,6},{6,7},{7,8},{8,9},{9,10},{10,1... | collective-permute-start | bytes 394760 | tf_op jit(solution)/shard_map/ppermute | solution.py:14
  327.7 2.7 fusion.56
  330.4 2.7 fusion.62
  333.1 2.7 fusion.59
  335.7 2.7 fusion.88
  338.4 11.9 %maximum_convert_fusion.1 = bf16[16,512,128]{2,1,0:T(8,128)(2,1)S(1)} fusion(f32[16,512,128]{2,1,0:T(8,128)} %fusion.53, f32[16,512,128]{2,1,0:T(8,128)} %fusion.56, f32[16,512,128]{2,1,0:T(8,128)} %fusion.116, f32[16,512,128]{2,1,0:T(8,128)} %fusion.142, f32[16,512,128]{2,1,0:T(8,128)} %fusion.118, f32[16,512,128]{2,1,0:T(8,128)} %fusion.88, ...), kind=kOutput, calls=%fused_computation.8 | convolution fusion | flops 284164096 | bytes 37947904 | tf_op jit(solution)/shard_map/dot_general | solution.py:28
  356.4 3.9 collective-permute-start.8
  361.6 2.7 fusion.112
  364.3 11.2 %collective-permute-done.9 = bf16[2,516,128]{2,1,0:T(8,128)(2,1)S(1)} collective-permute-done((bf16[2,516,128]{2,1,0:T(8,128)(2,1)S(1)}, bf16[2,516,128]{2,1,0:T(8,128)(2,1)S(1)}, u32[]{:S(2)}, u32[]{:S(2)}) %collective-permute-start.9) | collective-permute-done | bytes 264224 | tf_op jit(solution)/shard_map/ppermute | solution.py:15
  378.2 2.7 fusion.8
  380.9 2.7 fusion.14
  383.6 2.7 fusion.11
  386.2 2.7 fusion.82
  389.0 11.9 %maximum_convert_fusion = bf16[16,512,128]{2,1,0:T(8,128)(2,1)S(1)} fusion(f32[16,512,128]{2,1,0:T(8,128)} %fusion.5, f32[16,512,128]{2,1,0:T(8,128)} %fusion.8, f32[16,512,128]{2,1,0:T(8,128)} %fusion.112, f32[16,512,128]{2,1,0:T(8,128)} %fusion.141, f32[16,512,128]{2,1,0:T(8,128)} %fusion.114, f32[16,512,128]{2,1,0:T(8,128)} %fusion.82, ...), kind=kOutput, calls=%fused_computation.7 | convolution fusion | flops 284164096 | bytes 38081024 | tf_op jit(solution)/shard_map/dot_general | solution.py:28
  405.3 2.7 fusion.108
  408.6 4.6 collective-permute-start.10
  419.4 2.7 fusion.32
  423.8 2.7 fusion.38
  426.5 2.7 fusion.35
  429.2 2.7 fusion.78
  431.9 11.8 %add_convert_fusion = bf16[16,512,128]{2,1,0:T(8,128)(2,1)S(1)} fusion(f32[16,512,128]{2,1,0:T(8,128)} %fusion.29, f32[16,512,128]{2,1,0:T(8,128)} %fusion.32, f32[16,512,128]{2,1,0:T(8,128)} %fusion.108, f32[16,512,128]{2,1,0:T(8,128)} %fusion.140, f32[16,512,128]{2,1,0:T(8,128)} %fusion.110, f32[16,512,128]{2,1,0:T(8,128)} %fusion.78, ...), kind=kOutput, calls=%fused_computation.6 | convolution fusion | flops 285212672 | bytes 40444416 | tf_op jit(solution)/shard_map/dot_general | solution.py:28
  445.0 56.2 %all_to_all.56 = bf16[16,512,128]{2,0,1:T(8,128)(2,1)S(1)} all-to-all(bf16[16,512,128]{2,0,1:T(8,128)(2,1)S(1)} %copy.13), channel_id=1, replica_groups=mesh['row'=8,'col'=4] {'col'}, dimensions={1} | all-to-all | bytes 4194304 | tf_op jit(solution)/shard_map/all_to_all | solution.py:68
  (66 shorter events, 83.8 us)
Async XLA Ops:
  57.3 4.0 copy-start.2
  57.3 51.5 %all-to-all-start.1 = ((bf16[16,512,128]{2,0,1:T(8,128)(2,1)}), bf16[16,512,128]{2,0,1:T(8,128)(2,1)}, u32[]{:S(2)}, u32[]{:S(2)}) async-start(bf16[16,512,128]{2,0,1:T(8,128)(2,1)} %copy.9), calls=%async_computation.1 | async-start | bytes 4194304 | tf_op jit(solution)/shard_map/all_to_all | solution.py:65
  111.7 1.0 copy-start.1
  117.9 10.7 %collective-permute-start.1 = (bf16[1,514,128]{2,1,0:T(8,128)(2,1)S(1)}, bf16[1,514,128]{2,1,0:T(8,128)(2,1)S(1)}, u32[]{:S(2)}, u32[]{:S(2)}) collective-permute-start(bf16[1,514,128]{2,1,0:T(8,128)(2,1)S(1)} %get-tuple-element.8), channel_id=1, source_target_pairs={{1,0},{2,1},{3,2},{4,3},{5,4},{6,5},{7,6},{8,7},{9,8},{10,9},{11,1... | collective-permute-start | bytes 394760 | tf_op jit(solution)/shard_map/ppermute | solution.py:15
  121.9 12.1 %collective-permute-start = (bf16[1,514,128]{2,1,0:T(8,128)(2,1)S(1)}, bf16[1,514,128]{2,1,0:T(8,128)(2,1)S(1)}, u32[]{:S(2)}, u32[]{:S(2)}) collective-permute-start(bf16[1,514,128]{2,1,0:T(8,128)(2,1)S(1)} %get-tuple-element.7), channel_id=1, source_target_pairs={{0,1},{1,2},{2,3},{3,4},{4,5},{5,6},{6,7},{7,8},{8,9},{9,10},{10,1... | collective-permute-start | bytes 394760 | tf_op jit(solution)/shard_map/ppermute | solution.py:14
  154.1 1.0 copy-start
  160.4 23.8 %collective-permute-start.2 = (bf16[2,516,128]{2,1,0:T(8,128)(2,1)S(1)}, bf16[2,516,128]{2,1,0:T(8,128)(2,1)S(1)}, u32[]{:S(2)}, u32[]{:S(2)}) collective-permute-start(bf16[2,516,128]{2,1,0:T(8,128)(2,1)S(1)} %get-tuple-element.15), channel_id=1, source_target_pairs={{0,1},{1,2},{2,3},{3,4},{4,5},{5,6},{6,7},{7,8},{8,9},{9,10},{10,1... | collective-permute-start | bytes 792584 | tf_op jit(solution)/shard_map/ppermute | solution.py:14
  164.3 14.5 %collective-permute-start.3 = (bf16[2,516,128]{2,1,0:T(8,128)(2,1)S(1)}, bf16[2,516,128]{2,1,0:T(8,128)(2,1)S(1)}, u32[]{:S(2)}, u32[]{:S(2)}) collective-permute-start(bf16[2,516,128]{2,1,0:T(8,128)(2,1)S(1)} %get-tuple-element.16), channel_id=1, source_target_pairs={{1,0},{2,1},{3,2},{4,3},{5,4},{6,5},{7,6},{8,7},{9,8},{10,9},{11,1... | collective-permute-start | bytes 792584 | tf_op jit(solution)/shard_map/ppermute | solution.py:15
  204.4 16.0 %collective-permute-start.5 = (bf16[4,520,128]{2,1,0:T(8,128)(2,1)S(1)}, bf16[4,520,128]{2,1,0:T(8,128)(2,1)S(1)}, u32[]{:S(2)}, u32[]{:S(2)}) collective-permute-start(bf16[4,520,128]{2,1,0:T(8,128)(2,1)S(1)} %get-tuple-element.14), channel_id=1, source_target_pairs={{1,0},{2,1},{3,2},{4,3},{5,4},{6,5},{7,6},{8,7},{9,8},{10,9},{11,1... | collective-permute-start | bytes 1597448 | tf_op jit(solution)/shard_map/ppermute | solution.py:15
  211.6 15.7 %collective-permute-start.4 = (bf16[4,520,128]{2,1,0:T(8,128)(2,1)S(1)}, bf16[4,520,128]{2,1,0:T(8,128)(2,1)S(1)}, u32[]{:S(2)}, u32[]{:S(2)}) collective-permute-start(bf16[4,520,128]{2,1,0:T(8,128)(2,1)S(1)} %get-tuple-element.13), channel_id=1, source_target_pairs={{0,1},{1,2},{2,3},{3,4},{4,5},{5,6},{6,7},{7,8},{8,9},{9,10},{10,1... | collective-permute-start | bytes 1597448 | tf_op jit(solution)/shard_map/ppermute | solution.py:14
  314.4 10.6 %collective-permute-start.7 = (bf16[1,514,128]{2,1,0:T(8,128)(2,1)S(1)}, bf16[1,514,128]{2,1,0:T(8,128)(2,1)S(1)}, u32[]{:S(2)}, u32[]{:S(2)}) collective-permute-start(bf16[1,514,128]{2,1,0:T(8,128)(2,1)S(1)} %get-tuple-element.6), channel_id=1, source_target_pairs={{1,0},{2,1},{3,2},{4,3},{5,4},{6,5},{7,6},{8,7},{9,8},{10,9},{11,1... | collective-permute-start | bytes 394760 | tf_op jit(solution)/shard_map/ppermute | solution.py:15
  319.0 11.4 %collective-permute-start.6 = (bf16[1,514,128]{2,1,0:T(8,128)(2,1)S(1)}, bf16[1,514,128]{2,1,0:T(8,128)(2,1)S(1)}, u32[]{:S(2)}, u32[]{:S(2)}) collective-permute-start(bf16[1,514,128]{2,1,0:T(8,128)(2,1)S(1)} %get-tuple-element.5), channel_id=1, source_target_pairs={{0,1},{1,2},{2,3},{3,4},{4,5},{5,6},{6,7},{7,8},{8,9},{9,10},{10,1... | collective-permute-start | bytes 394760 | tf_op jit(solution)/shard_map/ppermute | solution.py:14
  356.4 24.5 %collective-permute-start.8 = (bf16[2,516,128]{2,1,0:T(8,128)(2,1)S(1)}, bf16[2,516,128]{2,1,0:T(8,128)(2,1)S(1)}, u32[]{:S(2)}, u32[]{:S(2)}) collective-permute-start(bf16[2,516,128]{2,1,0:T(8,128)(2,1)S(1)} %get-tuple-element.11), channel_id=1, source_target_pairs={{0,1},{1,2},{2,3},{3,4},{4,5},{5,6},{6,7},{7,8},{8,9},{9,10},{10,1... | collective-permute-start | bytes 792584 | tf_op jit(solution)/shard_map/ppermute | solution.py:14
  360.3 15.2 %collective-permute-start.9 = (bf16[2,516,128]{2,1,0:T(8,128)(2,1)S(1)}, bf16[2,516,128]{2,1,0:T(8,128)(2,1)S(1)}, u32[]{:S(2)}, u32[]{:S(2)}) collective-permute-start(bf16[2,516,128]{2,1,0:T(8,128)(2,1)S(1)} %get-tuple-element.12), channel_id=1, source_target_pairs={{1,0},{2,1},{3,2},{4,3},{5,4},{6,5},{7,6},{8,7},{9,8},{10,9},{11,1... | collective-permute-start | bytes 792584 | tf_op jit(solution)/shard_map/ppermute | solution.py:15
  401.2 15.5 %collective-permute-start.11 = (bf16[4,520,128]{2,1,0:T(8,128)(2,1)S(1)}, bf16[4,520,128]{2,1,0:T(8,128)(2,1)S(1)}, u32[]{:S(2)}, u32[]{:S(2)}) collective-permute-start(bf16[4,520,128]{2,1,0:T(8,128)(2,1)S(1)} %get-tuple-element.10), channel_id=1, source_target_pairs={{1,0},{2,1},{3,2},{4,3},{5,4},{6,5},{7,6},{8,7},{9,8},{10,9},{11,1... | collective-permute-start | bytes 1597448 | tf_op jit(solution)/shard_map/ppermute | solution.py:15
  408.6 15.3 %collective-permute-start.10 = (bf16[4,520,128]{2,1,0:T(8,128)(2,1)S(1)}, bf16[4,520,128]{2,1,0:T(8,128)(2,1)S(1)}, u32[]{:S(2)}, u32[]{:S(2)}) collective-permute-start(bf16[4,520,128]{2,1,0:T(8,128)(2,1)S(1)} %get-tuple-element.9), channel_id=1, source_target_pairs={{0,1},{1,2},{2,3},{3,4},{4,5},{5,6},{6,7},{7,8},{8,9},{9,10},{10,1... | collective-permute-start | bytes 1597448 | tf_op jit(solution)/shard_map/ppermute | solution.py:14
  429.2 2.7 copy-start.3
where the time goes:
time: 508 us; the launch traced here: 503 us
  matrix products  200 us (39%)
  blocking collectives  170 us (33%)
  waiting for transfers between devices  71.7 us (14%)
  starting transfers between devices  41.4 us (8%)
  local copies, waits for them, and re-layouts  18.3 us (4%)
    dot_general x54, matrix products, convolve(): jnp.dot(piece, kernel[tap_row, tap_col], preferred_element_type=jnp.float32)  200 us
    all_to_all x1, blocking collectives, per_device(): lax.all_to_all(current, ('row', 'col'), split_axis=1, concat_axis=0, tile...  59.4 us
    all_to_all x1, blocking collectives, per_device(): lax.all_to_all(current, 'col', split_axis=1, concat_axis=0, tiled=True)  56.2 us
    all_to_all x1, blocking collectives, per_device(): lax.all_to_all(contact_map, 'col', split_axis=0, concat_axis=1, tiled=True)  54.5 us
    all_to_all x1, waiting for transfers between devices, per_device(): lax.all_to_all(current, ('row', 'col'), split_axis=1, concat_axis=0, tile...  44.6 us
    ppermute x6, starting transfers between devices, with_halo(): before = lax.ppermute(last, axis, up)  29.4 us
    ppermute x6, waiting for transfers between devices, with_halo(): after = lax.ppermute(initial, axis, down)  23.8 us
  transfers between devices with their start and end apart: 13, of which 7 were waited for; matrix products, arithmetic and copies ran while one was open for 13% of the time, Pallas kernels for 0%

commit v1 on v0

--- a/solution.py
+++ b/solution.py
@@ -60,7 +60,15 @@
 
 def per_device(contact_map, conv_weight, conv_bias):
     blocks = conv_weight.shape[0]
-    current = lax.all_to_all(contact_map, "col", split_axis=0, concat_axis=1, tiled=True)
+    ways, here = (lax.axis_size("col"), lax.axis_index("col"))
+    width_2 = contact_map.shape[0] // ways
+    turned = jnp.roll(contact_map, -here * width_2, axis=0)
+    got = [lax.slice_in_dim(turned, 0, width_2, axis=0)]
+    for far in range(1, ways):
+        sent = lax.slice_in_dim(turned, far * width_2, (far + 1) * width_2, axis=0)
+        got.append(lax.ppermute(sent, "col", [(d, (d + far) % ways) for d in range(ways)]))
+    line = jnp.concatenate(got[::-1], axis=1)
+    current = jnp.roll(line, (here + 1) * got[0].shape[1], axis=1)
     for block in range(blocks):
         columns = lax.all_to_all(current, ("row", "col"), split_axis=1, concat_axis=0, tiled=True)
         flipped = jnp.transpose(columns, (1, 0, 2))

time: 508 us -> 514 us (1.012)
  blocking collectives: 170 us -> 116 us
  waiting for transfers between devices: 71.7 us -> 115 us
  starting transfers between devices: 41.4 us -> 48.6 us
  local copies, waits for them, and re-layouts: 18.3 us -> 24.3 us
    all_to_all x1 -> x0, blocking collectives: 54.5 us -> none  [per_device(): lax.all_to_all(contact_map, 'col', split_axis=0, concat_axis=1, tiled=True)]
    ppermute x0 -> x3, waiting for transfers between devices: none -> 43.9 us  [per_device(): lax.ppermute(sent, 'col', [(d, (d + far) % ways) for d in range(ways)])]
    unnamed x8 -> x19, local copies, waits for them, and re-layouts: 1.28 us -> 7.56 us
    ppermute x0 -> x3, starting transfers between devices: none -> 6.01 us  [per_device(): lax.ppermute(sent, 'col', [(d, (d + far) % ways) for d in range(ways)])]
  transfers between devices with their start and end apart: 13 -> 16, of which waited for: 7 -> 9; matrix products, arithmetic and copies ran while one was open for 13% -> 13% of each run, Pallas kernels for 0% -> 0%
where the time goes in v1:
time: 514 us; the launch traced here: 508 us
  matrix products  200 us (39%)
  blocking collectives  116 us (23%)
  waiting for transfers between devices  115 us (22%)
  starting transfers between devices  48.6 us (9%)
  local copies, waits for them, and re-layouts  24.3 us (5%)
    dot_general x54, matrix products, convolve(): jnp.dot(piece, kernel[tap_row, tap_col], preferred_element_type=jnp.float32)  200 us
    all_to_all x1, blocking collectives, per_device(): lax.all_to_all(current, ('row', 'col'), split_axis=1, concat_axis=0, tile...  59.4 us
    all_to_all x1, blocking collectives, per_device(): lax.all_to_all(current, 'col', split_axis=1, concat_axis=0, tiled=True)  56.1 us
    all_to_all x1, waiting for transfers between devices, per_device(): lax.all_to_all(current, ('row', 'col'), split_axis=1, concat_axis=0, tile...  44.6 us
    ppermute x3, waiting for transfers between devices, per_device(): lax.ppermute(sent, 'col', [(d, (d + far) % ways) for d in range(ways)])  43.9 us
    ppermute x6, starting transfers between devices, with_halo(): before = lax.ppermute(last, axis, up)  29.4 us
    ppermute x6, waiting for transfers between devices, with_halo(): after = lax.ppermute(initial, axis, down)  23.5 us
  transfers between devices with their start and end apart: 16, of which 9 were waited for; matrix products, arithmetic and copies ran while one was open for 13% of the time, Pallas kernels for 0%

profile of v1, /device:TPU:0, one launch (start us, length us, event | category | flops | bytes accessed | tf_op | source)
XLA Modules:
  0.0 508.4 jit_solution(198065559067813222)
XLA Ops:
  3.6 5.0 collective-permute-start
  9.6 11.7 %collective-permute-done = bf16[16,128,128]{2,1,0:T(8,128)(2,1)S(1)} collective-permute-done((bf16[16,128,128]{2,1,0:T(8,128)(2,1)}, bf16[16,128,128]{2,1,0:T(8,128)(2,1)S(1)}, u32[]{:S(2)}, u32[]{:S(2)}) %collective-permute-start) | collective-permute-done | bytes 524320 | tf_op jit(solution)/shard_map/ppermute | solution.py:69
  21.3 32.2 %collective-permute-done.1 = bf16[16,128,128]{2,1,0:T(8,128)(2,1)S(1)} collective-permute-done((bf16[16,128,128]{2,1,0:T(8,128)(2,1)}, bf16[16,128,128]{2,1,0:T(8,128)(2,1)S(1)}, u32[]{:S(2)}, u32[]{:S(2)}) %collective-permute-start.1) | collective-permute-done | bytes 524320 | tf_op jit(solution)/shard_map/ppermute | solution.py:69
  61.0 5.1 %all-to-all-start = ((bf16[16,512,128]{2,0,1:T(8,128)(2,1)}), bf16[16,512,128]{2,0,1:T(8,128)(2,1)S(1)}, u32[]{:S(2)}, u32[]{:S(2)}) async-start(bf16[16,512,128]{2,0,1:T(8,128)(2,1)} %copy.7), calls=%async_computation | async-start | bytes 4194304 | tf_op jit(solution)/shard_map/all_to_all | solution.py:73
  69.1 44.6 %all-to-all-done = bf16[16,512,128]{2,0,1:T(8,128)(2,1)S(1)} async-done(((bf16[16,512,128]{2,0,1:T(8,128)(2,1)}), bf16[16,512,128]{2,0,1:T(8,128)(2,1)S(1)}, u32[]{:S(2)}, u32[]{:S(2)}) %all-to-all-start) | async-done | bytes 2097184 | tf_op jit(solution)/shard_map/all_to_all | solution.py:73
  124.1 2.7 fusion.129
  126.8 6.2 %collective-permute-start.3 = (bf16[1,514,128]{2,1,0:T(8,128)(2,1)S(1)}, bf16[1,514,128]{2,1,0:T(8,128)(2,1)S(1)}, u32[]{:S(2)}, u32[]{:S(2)}) collective-permute-start(bf16[1,514,128]{2,1,0:T(8,128)(2,1)S(1)} %get-tuple-element.7), channel_id=1, source_target_pairs={{0,1},{1,2},{2,3},{3,4},{4,5},{5,6},{6,7},{7,8},{8,9},{9,10},{10,1... | collective-permute-start | bytes 394760 | tf_op jit(solution)/shard_map/ppermute | solution.py:14
  133.5 2.7 fusion.65
  136.2 2.7 fusion.68
  144.2 2.7 fusion.105
  147.0 11.9 %maximum_convert_fusion.3 = bf16[16,512,128]{2,1,0:T(8,128)(2,1)S(1)} fusion(f32[16,512,128]{2,1,0:T(8,128)} %fusion.65, f32[16,512,128]{2,1,0:T(8,128)} %fusion.68, f32[16,512,128]{2,1,0:T(8,128)} %fusion.129, f32[16,512,128]{2,1,0:T(8,128)} %fusion.146, f32[16,512,128]{2,1,0:T(8,128)} %fusion.131, f32[16,512,128]{2,1,0:T(8,128)} %fusion.105, ...), kind=kOutput, calls=%fused_computation.13 | convolution fusion | flops 284164096 | bytes 37947904 | tf_op jit(solution)/shard_map/dot_general | solution.py:28
  165.3 3.9 collective-permute-start.5
  170.7 2.7 fusion.125
  173.4 10.3 %collective-permute-done.6 = bf16[2,516,128]{2,1,0:T(8,128)(2,1)S(1)} collective-permute-done((bf16[2,516,128]{2,1,0:T(8,128)(2,1)S(1)}, bf16[2,516,128]{2,1,0:T(8,128)(2,1)S(1)}, u32[]{:S(2)}, u32[]{:S(2)}) %collective-permute-start.6) | collective-permute-done | bytes 264224 | tf_op jit(solution)/shard_map/ppermute | solution.py:15
  186.4 2.7 fusion.20
  189.1 2.7 fusion.26
  194.5 2.7 fusion.99
  197.2 11.9 %maximum_convert_fusion.2 = bf16[16,512,128]{2,1,0:T(8,128)(2,1)S(1)} fusion(f32[16,512,128]{2,1,0:T(8,128)} %fusion.17, f32[16,512,128]{2,1,0:T(8,128)} %fusion.20, f32[16,512,128]{2,1,0:T(8,128)} %fusion.125, f32[16,512,128]{2,1,0:T(8,128)} %fusion.145, f32[16,512,128]{2,1,0:T(8,128)} %fusion.127, f32[16,512,128]{2,1,0:T(8,128)} %fusion.99, ...), kind=kOutput, calls=%fused_computation.12 | convolution fusion | flops 284164096 | bytes 38081024 | tf_op jit(solution)/shard_map/dot_general | solution.py:28
  213.4 2.7 fusion.121
  216.7 4.8 collective-permute-start.7
  228.0 2.7 fusion.44
  232.4 2.7 fusion.50
  237.8 2.7 fusion.95
  240.5 11.8 %add_convert_fusion.1 = bf16[16,512,128]{2,1,0:T(8,128)(2,1)S(1)} fusion(f32[16,512,128]{2,1,0:T(8,128)} %fusion.41, f32[16,512,128]{2,1,0:T(8,128)} %fusion.44, f32[16,512,128]{2,1,0:T(8,128)} %fusion.121, f32[16,512,128]{2,1,0:T(8,128)} %fusion.144, f32[16,512,128]{2,1,0:T(8,128)} %fusion.123, f32[16,512,128]{2,1,0:T(8,128)} %fusion.95, ...), kind=kOutput, calls=%fused_computation.11 | convolution fusion | flops 285212672 | bytes 40444416 | tf_op jit(solution)/shard_map/dot_general | solution.py:28
  253.6 59.4 %all_to_all.36 = bf16[16,512,128]{2,0,1:T(8,128)(2,1)S(1)} all-to-all(bf16[16,512,128]{2,0,1:T(8,128)(2,1)S(1)} %copy.9), channel_id=1, replica_groups=mesh['row'=8,'col'=4] {'row','col'}, dimensions={1} | all-to-all | bytes 4194304 | tf_op jit(solution)/shard_map/all_to_all | solution.py:73
  320.8 2.7 fusion.117
  324.0 6.0 %collective-permute-start.9 = (bf16[1,514,128]{2,1,0:T(8,128)(2,1)S(1)}, bf16[1,514,128]{2,1,0:T(8,128)(2,1)S(1)}, u32[]{:S(2)}, u32[]{:S(2)}) collective-permute-start(bf16[1,514,128]{2,1,0:T(8,128)(2,1)S(1)} %get-tuple-element.5), channel_id=1, source_target_pairs={{0,1},{1,2},{2,3},{3,4},{4,5},{5,6},{6,7},{7,8},{8,9},{9,10},{10,1... | collective-permute-start | bytes 394760 | tf_op jit(solution)/shard_map/ppermute | solution.py:14
  330.1 2.7 fusion.53
  332.8 2.7 fusion.56
  335.5 2.7 fusion.62
  340.9 2.7 fusion.89
  343.6 11.9 %maximum_convert_fusion.1 = bf16[16,512,128]{2,1,0:T(8,128)(2,1)S(1)} fusion(f32[16,512,128]{2,1,0:T(8,128)} %fusion.53, f32[16,512,128]{2,1,0:T(8,128)} %fusion.56, f32[16,512,128]{2,1,0:T(8,128)} %fusion.117, f32[16,512,128]{2,1,0:T(8,128)} %fusion.143, f32[16,512,128]{2,1,0:T(8,128)} %fusion.119, f32[16,512,128]{2,1,0:T(8,128)} %fusion.89, ...), kind=kOutput, calls=%fused_computation.10 | convolution fusion | flops 284164096 | bytes 37947904 | tf_op jit(solution)/shard_map/dot_general | solution.py:28
  361.6 3.9 collective-permute-start.11
  366.8 2.7 fusion.113
  369.5 11.2 %collective-permute-done.12 = bf16[2,516,128]{2,1,0:T(8,128)(2,1)S(1)} collective-permute-done((bf16[2,516,128]{2,1,0:T(8,128)(2,1)S(1)}, bf16[2,516,128]{2,1,0:T(8,128)(2,1)S(1)}, u32[]{:S(2)}, u32[]{:S(2)}) %collective-permute-start.12) | collective-permute-done | bytes 264224 | tf_op jit(solution)/shard_map/ppermute | solution.py:15
  383.3 2.7 fusion.8
  386.0 2.7 fusion.14
  388.7 2.7 fusion.11
  391.4 2.7 fusion.83
  394.1 11.9 %maximum_convert_fusion = bf16[16,512,128]{2,1,0:T(8,128)(2,1)S(1)} fusion(f32[16,512,128]{2,1,0:T(8,128)} %fusion.5, f32[16,512,128]{2,1,0:T(8,128)} %fusion.8, f32[16,512,128]{2,1,0:T(8,128)} %fusion.113, f32[16,512,128]{2,1,0:T(8,128)} %fusion.142, f32[16,512,128]{2,1,0:T(8,128)} %fusion.115, f32[16,512,128]{2,1,0:T(8,128)} %fusion.83, ...), kind=kOutput, calls=%fused_computation.9 | convolution fusion | flops 284164096 | bytes 38081024 | tf_op jit(solution)/shard_map/dot_general | solution.py:28
  410.5 2.7 fusion.109
  413.8 4.6 collective-permute-start.13
  421.9 2.7 fusion.29
  424.6 2.7 fusion.32
  429.0 2.7 fusion.38
  434.4 2.7 fusion.79
  437.1 11.8 %add_convert_fusion = bf16[16,512,128]{2,1,0:T(8,128)(2,1)S(1)} fusion(f32[16,512,128]{2,1,0:T(8,128)} %fusion.29, f32[16,512,128]{2,1,0:T(8,128)} %fusion.32, f32[16,512,128]{2,1,0:T(8,128)} %fusion.109, f32[16,512,128]{2,1,0:T(8,128)} %fusion.141, f32[16,512,128]{2,1,0:T(8,128)} %fusion.111, f32[16,512,128]{2,1,0:T(8,128)} %fusion.79, ...), kind=kOutput, calls=%fused_computation.8 | convolution fusion | flops 285212672 | bytes 40444416 | tf_op jit(solution)/shard_map/dot_general | solution.py:28
  450.2 56.1 %all_to_all.37 = bf16[16,512,128]{2,0,1:T(8,128)(2,1)S(1)} all-to-all(bf16[16,512,128]{2,0,1:T(8,128)(2,1)S(1)} %copy.11), channel_id=1, replica_groups=mesh['row'=8,'col'=4] {'col'}, dimensions={1} | all-to-all | bytes 4194304 | tf_op jit(solution)/shard_map/all_to_all | solution.py:76
  (85 shorter events, 98.6 us)
Async XLA Ops:
  3.6 17.7 %collective-permute-start = (bf16[16,128,128]{2,1,0:T(8,128)(2,1)}, bf16[16,128,128]{2,1,0:T(8,128)(2,1)S(1)}, u32[]{:S(2)}, u32[]{:S(2)}) collective-permute-start(bf16[16,128,128]{2,1,0:T(8,128)(2,1)} %get-tuple-element.19), channel_id=1, source_target_pairs={{0,3},{1,0},{2,1},{3,2},{4,7},{5,4},{6,5},{7,6},{8,11},{9,8},{10,9... | collective-permute-start | bytes 1572872 | tf_op jit(solution)/shard_map/ppermute | solution.py:69
  8.6 44.9 %collective-permute-start.1 = (bf16[16,128,128]{2,1,0:T(8,128)(2,1)}, bf16[16,128,128]{2,1,0:T(8,128)(2,1)S(1)}, u32[]{:S(2)}, u32[]{:S(2)}) collective-permute-start(bf16[16,128,128]{2,1,0:T(8,128)(2,1)} %get-tuple-element.18), channel_id=1, source_target_pairs={{0,2},{1,3},{2,0},{3,1},{4,6},{5,7},{6,4},{7,5},{8,10},{9,11},{10,... | collective-permute-start | bytes 1572872 | tf_op jit(solution)/shard_map/ppermute | solution.py:69
  8.6 45.0 %collective-permute-start.2 = (bf16[16,128,128]{2,1,0:T(8,128)(2,1)}, bf16[16,128,128]{2,1,0:T(8,128)(2,1)}, u32[]{:S(2)}, u32[]{:S(2)}) collective-permute-start(bf16[16,128,128]{2,1,0:T(8,128)(2,1)} %get-tuple-element.17), channel_id=1, source_target_pairs={{0,1},{1,2},{2,3},{3,0},{4,5},{5,6},{6,7},{7,4},{8,9},{9,10},{10,1... | collective-permute-start | bytes 1572872 | tf_op jit(solution)/shard_map/ppermute | solution.py:69
  56.2 2.0 copy-start
  61.0 5.1 %copy-start.4 = (f32[2,3,128]{2,0,1:T(2,128)S(1)}, f32[2,3,128]{2,0,1:T(2,128)}, u32[]{:S(2)}) copy-start(f32[2,3,128]{2,0,1:T(2,128)} %param.5) | copy-start | bytes 9220
  61.0 52.6 %all-to-all-start = ((bf16[16,512,128]{2,0,1:T(8,128)(2,1)}), bf16[16,512,128]{2,0,1:T(8,128)(2,1)S(1)}, u32[]{:S(2)}, u32[]{:S(2)}) async-start(bf16[16,512,128]{2,0,1:T(8,128)(2,1)} %copy.7), calls=%async_computation | async-start | bytes 4194304 | tf_op jit(solution)/shard_map/all_to_all | solution.py:73
  113.7 2.2 copy-start.1
  116.5 1.0 copy-start.3
  122.8 10.7 %collective-permute-start.4 = (bf16[1,514,128]{2,1,0:T(8,128)(2,1)S(1)}, bf16[1,514,128]{2,1,0:T(8,128)(2,1)S(1)}, u32[]{:S(2)}, u32[]{:S(2)}) collective-permute-start(bf16[1,514,128]{2,1,0:T(8,128)(2,1)S(1)} %get-tuple-element.8), channel_id=1, source_target_pairs={{1,0},{2,1},{3,2},{4,3},{5,4},{6,5},{7,6},{8,7},{9,8},{10,9},{11,1... | collective-permute-start | bytes 394760 | tf_op jit(solution)/shard_map/ppermute | solution.py:15
  126.8 12.1 %collective-permute-start.3 = (bf16[1,514,128]{2,1,0:T(8,128)(2,1)S(1)}, bf16[1,514,128]{2,1,0:T(8,128)(2,1)S(1)}, u32[]{:S(2)}, u32[]{:S(2)}) collective-permute-start(bf16[1,514,128]{2,1,0:T(8,128)(2,1)S(1)} %get-tuple-element.7), channel_id=1, source_target_pairs={{0,1},{1,2},{2,3},{3,4},{4,5},{5,6},{6,7},{7,8},{8,9},{9,10},{10,1... | collective-permute-start | bytes 394760 | tf_op jit(solution)/shard_map/ppermute | solution.py:14
  159.1 1.0 copy-start.2
  165.3 23.8 %collective-permute-start.5 = (bf16[2,516,128]{2,1,0:T(8,128)(2,1)S(1)}, bf16[2,516,128]{2,1,0:T(8,128)(2,1)S(1)}, u32[]{:S(2)}, u32[]{:S(2)}) collective-permute-start(bf16[2,516,128]{2,1,0:T(8,128)(2,1)S(1)} %get-tuple-element.15), channel_id=1, source_target_pairs={{0,1},{1,2},{2,3},{3,4},{4,5},{5,6},{6,7},{7,8},{8,9},{9,10},{10,1... | collective-permute-start | bytes 792584 | tf_op jit(solution)/shard_map/ppermute | solution.py:14
  169.3 14.4 %collective-permute-start.6 = (bf16[2,516,128]{2,1,0:T(8,128)(2,1)S(1)}, bf16[2,516,128]{2,1,0:T(8,128)(2,1)S(1)}, u32[]{:S(2)}, u32[]{:S(2)}) collective-permute-start(bf16[2,516,128]{2,1,0:T(8,128)(2,1)S(1)} %get-tuple-element.16), channel_id=1, source_target_pairs={{1,0},{2,1},{3,2},{4,3},{5,4},{6,5},{7,6},{8,7},{9,8},{10,9},{11,1... | collective-permute-start | bytes 792584 | tf_op jit(solution)/shard_map/ppermute | solution.py:15
  209.4 15.9 %collective-permute-start.8 = (bf16[4,520,128]{2,1,0:T(8,128)(2,1)S(1)}, bf16[4,520,128]{2,1,0:T(8,128)(2,1)S(1)}, u32[]{:S(2)}, u32[]{:S(2)}) collective-permute-start(bf16[4,520,128]{2,1,0:T(8,128)(2,1)S(1)} %get-tuple-element.14), channel_id=1, source_target_pairs={{1,0},{2,1},{3,2},{4,3},{5,4},{6,5},{7,6},{8,7},{9,8},{10,9},{11,1... | collective-permute-start | bytes 1597448 | tf_op jit(solution)/shard_map/ppermute | solution.py:15
  216.7 15.7 %collective-permute-start.7 = (bf16[4,520,128]{2,1,0:T(8,128)(2,1)S(1)}, bf16[4,520,128]{2,1,0:T(8,128)(2,1)S(1)}, u32[]{:S(2)}, u32[]{:S(2)}) collective-permute-start(bf16[4,520,128]{2,1,0:T(8,128)(2,1)S(1)} %get-tuple-element.13), channel_id=1, source_target_pairs={{0,1},{1,2},{2,3},{3,4},{4,5},{5,6},{6,7},{7,8},{8,9},{9,10},{10,1... | collective-permute-start | bytes 1597448 | tf_op jit(solution)/shard_map/ppermute | solution.py:14
  319.5 10.6 %collective-permute-start.10 = (bf16[1,514,128]{2,1,0:T(8,128)(2,1)S(1)}, bf16[1,514,128]{2,1,0:T(8,128)(2,1)S(1)}, u32[]{:S(2)}, u32[]{:S(2)}) collective-permute-start(bf16[1,514,128]{2,1,0:T(8,128)(2,1)S(1)} %get-tuple-element.6), channel_id=1, source_target_pairs={{1,0},{2,1},{3,2},{4,3},{5,4},{6,5},{7,6},{8,7},{9,8},{10,9},{11,1... | collective-permute-start | bytes 394760 | tf_op jit(solution)/shard_map/ppermute | solution.py:15
  324.0 11.5 %collective-permute-start.9 = (bf16[1,514,128]{2,1,0:T(8,128)(2,1)S(1)}, bf16[1,514,128]{2,1,0:T(8,128)(2,1)S(1)}, u32[]{:S(2)}, u32[]{:S(2)}) collective-permute-start(bf16[1,514,128]{2,1,0:T(8,128)(2,1)S(1)} %get-tuple-element.5), channel_id=1, source_target_pairs={{0,1},{1,2},{2,3},{3,4},{4,5},{5,6},{6,7},{7,8},{8,9},{9,10},{10,1... | collective-permute-start | bytes 394760 | tf_op jit(solution)/shard_map/ppermute | solution.py:14
  361.6 24.5 %collective-permute-start.11 = (bf16[2,516,128]{2,1,0:T(8,128)(2,1)S(1)}, bf16[2,516,128]{2,1,0:T(8,128)(2,1)S(1)}, u32[]{:S(2)}, u32[]{:S(2)}) collective-permute-start(bf16[2,516,128]{2,1,0:T(8,128)(2,1)S(1)} %get-tuple-element.11), channel_id=1, source_target_pairs={{0,1},{1,2},{2,3},{3,4},{4,5},{5,6},{6,7},{7,8},{8,9},{9,10},{10,1... | collective-permute-start | bytes 792584 | tf_op jit(solution)/shard_map/ppermute | solution.py:14
  365.5 15.2 %collective-permute-start.12 = (bf16[2,516,128]{2,1,0:T(8,128)(2,1)S(1)}, bf16[2,516,128]{2,1,0:T(8,128)(2,1)S(1)}, u32[]{:S(2)}, u32[]{:S(2)}) collective-permute-start(bf16[2,516,128]{2,1,0:T(8,128)(2,1)S(1)} %get-tuple-element.12), channel_id=1, source_target_pairs={{1,0},{2,1},{3,2},{4,3},{5,4},{6,5},{7,6},{8,7},{9,8},{10,9},{11,1... | collective-permute-start | bytes 792584 | tf_op jit(solution)/shard_map/ppermute | solution.py:15
  406.4 15.5 %collective-permute-start.14 = (bf16[4,520,128]{2,1,0:T(8,128)(2,1)S(1)}, bf16[4,520,128]{2,1,0:T(8,128)(2,1)S(1)}, u32[]{:S(2)}, u32[]{:S(2)}) collective-permute-start(bf16[4,520,128]{2,1,0:T(8,128)(2,1)S(1)} %get-tuple-element.10), channel_id=1, source_target_pairs={{1,0},{2,1},{3,2},{4,3},{5,4},{6,5},{7,6},{8,7},{9,8},{10,9},{11,1... | collective-permute-start | bytes 1597448 | tf_op jit(solution)/shard_map/ppermute | solution.py:15
  413.8 15.2 %collective-permute-start.13 = (bf16[4,520,128]{2,1,0:T(8,128)(2,1)S(1)}, bf16[4,520,128]{2,1,0:T(8,128)(2,1)S(1)}, u32[]{:S(2)}, u32[]{:S(2)}) collective-permute-start(bf16[4,520,128]{2,1,0:T(8,128)(2,1)S(1)} %get-tuple-element.9), channel_id=1, source_target_pairs={{0,1},{1,2},{2,3},{3,4},{4,5},{5,6},{6,7},{7,8},{8,9},{9,10},{10,1... | collective-permute-start | bytes 1597448 | tf_op jit(solution)/shard_map/ppermute | solution.py:14
  434.4 2.7 copy-start.5
